TPU v7x, 256 devices: a whole 4x4x8 slice. The times are simulated.
256 devices in a mesh: frame: 16 (over z, core), tok: 16 (over x, y).
Axes of the slice: x: 4, y: 4, z: 8, core: 2. Of those that a mesh axis runs over, the one named last changes fastest.
Arguments:
- stream: bfloat16 [16, 4096, 1152], P('frame', 'tok'), may hold values from -20 to 20
- queries: bfloat16 [16, 4096, 1152], P('frame', 'tok'), may hold values from -200 to 200
- key_vectors: bfloat16 [16, 4096, 1152], P('frame', 'tok'), may hold values from -6 to 6
- value_vectors: bfloat16 [16, 4096, 1152], P('frame', 'tok'), may hold values from -6 to 6
- modulation: float32 [16, 4, 1152], P('frame'), may hold values from -4 to 4
- output_weight: bfloat16 [1152, 1152], replicated, may hold values from -0.1875 to 0.1875
- output_bias: float32 [1152], replicated, may hold values from -3 to 3
- router_weight: bfloat16 [1152, 16], replicated, may hold values from -0.1875 to 0.1875
- expand_weight: bfloat16 [16, 1152, 4608], P('frame', None, 'tok'), may hold values from -0.1875 to 0.1875
- expand_bias: float32 [16, 4608], P('frame', 'tok'), may hold values from -3 to 3
- reduce_weight: bfloat16 [16, 4608, 1152], P('frame', 'tok'), may hold values from -0.09375 to 0.09375
- reduce_bias: float32 [16, 1152], P('frame'), may hold values from -3 to 3
- counts: int32 [16, 16], P(None, 'frame'), may hold values from 1 to 48, 256 in all within a row
- picked_rows: int32 [16, 16, 48], P(None, 'frame'), may hold values from 0 to 4095, as said below
Outputs:
- layer_out: bfloat16 [16, 4096, 1152], P('frame', 'tok')
Inputs may be any that keep to these rules, and one draw needn't show every extreme that they name: counts[e, g] slots of block (e, g) are used; the counts of one expert sum to 256. The entries of one block picked_rows[e, g, :] are distinct positions among the 4096 tokens of frame g; slots at or beyond counts[e, g] are unused.
All inputs are finite; a program needn't handle non-finite values.
Results may differ from a plain program's by a relative error of at most 0.0055.
Values may be sent and summed in bfloat16 or wider, within the bound.
No kernel may reach another device: no remote copies, remote signals or barrier semaphores. Data moves between devices by JAX's collectives and lax.ppermute only.
A program may use at most 64 MiB of HBM per device.

v0:
```python
import math
import jax
import jax.numpy as jnp
from jax import lax
from jax.sharding import PartitionSpec as P

H = 16
HD = 72


def layer_norm(values):
    mean_val = jnp.mean(values, axis=-1, keepdims=True)
    centred = values - mean_val
    variance = jnp.mean(centred * centred, axis=-1, keepdims=True)
    return centred * lax.rsqrt(variance + 1e-06)


def head_attention(operands):
    head_queries, head_keys, head_values = operands
    length = head_queries.shape[1]
    block_rows = min(512, length)
    score_scale = 1.0 / math.sqrt(HD)

    def one_block(first_row):
        query_block = lax.dynamic_slice_in_dim(head_queries, first_row, block_rows, 1)
        scores = (
            lax.dot_general(
                query_block, head_keys, (((0,), (0,)), ((), ())), preferred_element_type=jnp.float32
            )
            * score_scale
        )
        scores = scores - jnp.max(scores, axis=1, keepdims=True)
        exponent = jnp.exp(scores)
        weights = (exponent / jnp.sum(exponent, axis=1, keepdims=True)).astype(jnp.bfloat16)
        return lax.dot_general(
            head_values, weights, (((1,), (1,)), ((), ())), preferred_element_type=jnp.float32
        ).astype(jnp.bfloat16)

    starts = jnp.arange(length // block_rows, dtype=jnp.int32) * block_rows
    blocks = lax.map(one_block, starts)
    return blocks.transpose(1, 0, 2).reshape(head_queries.shape[0], length)


def attend_items(pieces):
    outputs = lax.map(head_attention, (pieces[0][0], pieces[1][0], pieces[2][0]))
    return outputs[None]


def per_device(
    stream,
    queries,
    key_vectors,
    value_vectors,
    modulation,
    output_weight,
    output_bias,
    router_weight,
    expand_weight,
    expand_bias,
    reduce_weight,
    reduce_bias,
    counts,
    picked_rows,
):
    tok_groups = lax.axis_size("tok")
    tok_local = stream.shape[1]
    model_width = stream.shape[2]
    heads_local = H // tok_groups

    def to_heads(tensor):
        return tensor[0].reshape(tok_local, tok_groups, heads_local, HD).transpose(1, 2, 3, 0)

    attended = attend_items(
        (
            lax.all_to_all(to_heads(queries), "tok", split_axis=0, concat_axis=3, tiled=True),
            lax.all_to_all(to_heads(key_vectors), "tok", split_axis=0, concat_axis=3, tiled=True),
            lax.all_to_all(to_heads(value_vectors), "tok", split_axis=0, concat_axis=3, tiled=True),
        )
    )
    returned = lax.all_to_all(attended, "tok", split_axis=3, concat_axis=0, tiled=True)
    attended_rows = returned.transpose(3, 0, 1, 2).reshape(tok_local, model_width)
    projected = (
        jnp.dot(attended_rows, output_weight, preferred_element_type=jnp.float32) + output_bias
    )
    shares = modulation[0]
    residual = (stream[0].astype(jnp.float32) + shares[0] * projected).astype(jnp.bfloat16)
    normed = (layer_norm(residual.astype(jnp.float32)) * (1.0 + shares[2]) + shares[1]).astype(
        jnp.bfloat16
    )
    gate_values = jax.nn.sigmoid(jnp.dot(normed, router_weight, preferred_element_type=jnp.float32))
    slot_count = picked_rows.shape[2]
    local_pos = picked_rows[:, 0, :] - lax.axis_index("tok") * tok_local
    in_use = jnp.arange(slot_count, dtype=jnp.int32)[None, :] < counts
    on_shard = in_use & (local_pos >= 0) & (local_pos < tok_local)
    safe_pos = jnp.clip(local_pos, 0, tok_local - 1)
    chosen = jnp.take(normed, safe_pos, axis=0)
    chosen = jnp.where(on_shard[:, :, None], chosen, jnp.zeros_like(chosen))
    moved = lax.all_to_all(chosen, "frame", split_axis=0, concat_axis=1, tiled=True)
    expert_rows = lax.psum(moved.astype(jnp.float32).astype(jnp.bfloat16), "tok")
    hidden = jax.nn.gelu(
        jnp.einsum("erd,edf->erf", expert_rows, expand_weight, preferred_element_type=jnp.float32)
        + expand_bias[:, None, :],
        approximate=True,
    ).astype(jnp.bfloat16)
    partial_out = jnp.einsum(
        "erf,efd->erd", hidden, reduce_weight, preferred_element_type=jnp.float32
    )
    summed = lax.psum(partial_out.astype(jnp.bfloat16), "tok").astype(jnp.float32)
    expert_out = (summed + reduce_bias[:, None, :]).astype(jnp.bfloat16)
    returned_rows = lax.all_to_all(expert_out, "frame", split_axis=1, concat_axis=0, tiled=True)
    mix_weight = jnp.take_along_axis(gate_values.T, safe_pos, axis=1)
    mix_weight = jnp.where(on_shard, mix_weight, jnp.zeros_like(mix_weight)).astype(jnp.bfloat16)
    targets = jnp.arange(tok_local, dtype=jnp.int32)
    matches = (safe_pos.reshape(-1)[None, :] == targets[:, None]) & on_shard.reshape(-1)[None, :]
    scatter_table = jnp.where(matches, mix_weight.reshape(-1)[None, :], jnp.zeros((), jnp.bfloat16))
    expert_mix = jnp.dot(
        scatter_table, returned_rows.reshape(-1, model_width), preferred_element_type=jnp.float32
    )
    layer_out = (residual.astype(jnp.float32) + shares[3] * expert_mix).astype(jnp.bfloat16)
    return layer_out[None]


def solution(mesh):
    return jax.shard_map(
        per_device,
        mesh=mesh,
        in_specs=(
            P("frame", "tok", None),
            P("frame", "tok", None),
            P("frame", "tok", None),
            P("frame", "tok", None),
            P("frame", None, None),
            P(),
            P(),
            P(),
            P("frame", None, "tok"),
            P("frame", "tok"),
            P("frame", "tok", None),
            P("frame", None),
            P(None, "frame"),
            P(None, "frame", None),
        ),
        out_specs=P("frame", "tok", None),
        check_vma=False,
    )
```

profile of v0, /device:TPU:1, one launch (start us, length us, event | category | flops | bytes accessed | tf_op | source)
XLA Modules:
  0.0 551.0 jit_solution(5295147345059921114)
XLA Ops:
  8.8 7.6 %all-to-all-start = ((bf16[16,1,72,256]{3,2,1,0:T(8,128)(2,1)}), bf16[16,1,72,256]{3,2,1,0:T(8,128)(2,1)S(1)}, u32[]{:S(2)}, u32[]{:S(2)}) async-start(bf16[16,1,72,256]{3,2,1,0:T(8,128)(2,1)} %bitcast.139), calls=%async_computation | async-start | bytes 1179648 | tf_op jit(solution)/shard_map/all_to_all | solution.py:75
  18.5 8.9 %all-to-all-done = bf16[16,1,72,256]{3,2,1,0:T(8,128)(2,1)S(1)} async-done(((bf16[16,1,72,256]{3,2,1,0:T(8,128)(2,1)}), bf16[16,1,72,256]{3,2,1,0:T(8,128)(2,1)S(1)}, u32[]{:S(2)}, u32[]{:S(2)}) %all-to-all-start) | async-done | bytes 589856 | tf_op jit(solution)/shard_map/all_to_all | solution.py:75
  27.4 4.4 all-to-all-start.1
  33.9 7.3 %all-to-all-done.1 = bf16[16,1,72,256]{3,2,1,0:T(8,128)(2,1)} async-done(((bf16[16,1,72,256]{3,2,1,0:T(8,128)(2,1)}), bf16[16,1,72,256]{3,2,1,0:T(8,128)(2,1)}, u32[]{:S(2)}, u32[]{:S(2)}) %all-to-all-start.1) | async-done | bytes 589856 | tf_op jit(solution)/shard_map/all_to_all | solution.py:76
  41.2 4.7 all-to-all-start.2
  48.1 7.2 %all-to-all-done.2 = bf16[16,1,72,256]{3,2,1,0:T(8,128)(2,1)} async-done(((bf16[16,1,72,256]{3,2,1,0:T(8,128)(2,1)}), bf16[16,1,72,256]{3,2,1,0:T(8,128)(2,1)}, u32[]{:S(2)}, u32[]{:S(2)}) %all-to-all-start.2) | async-done | bytes 589856 | tf_op jit(solution)/shard_map/all_to_all | solution.py:77
  57.3 74.4 %while.17 = (s32[]{:T(128)}, bf16[8,72,512]{2,1,0:T(8,128)(2,1)}, s32[8]{0:T(128)S(1)}, bf16[72,4096]{1,0:T(8,128)(2,1)}, bf16[72,4096]{1,0:T(8,128)(2,1)S(1)}, ...) while((s32[]{:T(128)}, bf16[8,72,512]{2,1,0:T(8,128)(2,1)}, s32[8]{0:T(128)S(1)}, ...), condition=%wide.region_3.0_spmd, body=%wide.region_0.3_spmd.sunk | while | flops 622889984 | bytes 28862648 | solution.py:40
  133.9 6.9 %reshape.245 = bf16[1,1,72,4096]{2,1,0,3:T(2,128)(2,1)} reshape(bf16[72,8,512]{0,2,1:T(8,128)(2,1)} %copy.78) | data formatting | bytes 1179648 | tf_op jit(solution)/shard_map/broadcast_in_dim | solution.py:46
  141.3 24.4 %reduce.12 = bf16[4096,72]{1,0:T(8,128)(2,1)} reduce(bf16[4096,1,1,72]{3,2,1,0:T(2,128)(2,1)} %bitcast.131, bf16[]{:T(256)} %broadcast.275), dimensions={1,2}, to_apply=%bitcast.108.reduce_sub_computation | reduce | bytes 1179650
  165.8 4.3 reshape.253
  173.9 9.1 %all-to-all-done.3 = bf16[16,2,9216]{2,1,0:T(2,128)(2,1)S(1)} async-done(((bf16[16,2,9216]{2,1,0:T(2,128)(2,1)}), bf16[16,2,9216]{2,1,0:T(2,128)(2,1)S(1)}, u32[]{:S(2)}, u32[]{:S(2)}) %all-to-all-start.3) | async-done | bytes 589856 | tf_op jit(solution)/shard_map/all_to_all | solution.py:80
  183.0 5.1 reshape.254
  188.1 4.6 copy.73
  201.8 57.8 %all_to_all.84 = bf16[16,48,1152]{2,1,0:T(8,128)(2,1)} all-to-all(bf16[16,48,1152]{2,1,0:T(8,128)(2,1)S(1)} %select_select_fusion), channel_id=1, replica_groups=mesh['frame'=16,'tok'=16] {'frame'}, dimensions={0} | all-to-all | bytes 3538944 | tf_op jit(solution)/shard_map/all_to_all | solution.py:98
  260.3 90.5 %all-reduce.3.cloned.1.call-done = bf16[768,1152]{1,0:T(8,128)(2,1)} async-done(((bf16[768,1152]{1,0:T(8,128)(2,1)}), bf16[768,1152]{1,0:T(8,128)(2,1)}) %all-reduce.3.cloned.1.call-update) | async-done | bytes 1769488 | tf_op jit(solution)/shard_map/psum | solution.py:99
  350.8 5.3 fusion.9
  356.7 98.2 %all-reduce.5.cloned.1.call-done = bf16[1,768,1152]{2,1,0:T(8,128)(2,1)} async-done(((bf16[1,768,1152]{2,1,0:T(8,128)(2,1)}), bf16[1,768,1152]{2,1,0:T(8,128)(2,1)}) %all-reduce.5.cloned.1.call-update) | async-done | bytes 1769488 | tf_op jit(solution)/shard_map/psum | solution.py:108
  456.7 4.5 copy.95
  461.2 12.6 %reduce.13 = bf16[768,1152]{1,0:T(8,128)(2,1)} reduce(bf16[768,1,1152]{2,1,0:T(2,128)(2,1)} %bitcast.130, bf16[]{:T(256)} %broadcast.275), dimensions={1}, to_apply=%bitcast.120.reduce_sub_computation | reduce | bytes 3538946
  473.8 4.7 reshape.255
  478.5 9.2 %all-to-all-start.5 = ((bf16[16,2,27648]{2,1,0:T(2,128)(2,1)}), bf16[16,2,27648]{2,1,0:T(2,128)(2,1)}, u32[]{:S(2)}, u32[]{:S(2)}) async-start(bf16[16,2,27648]{2,1,0:T(2,128)(2,1)} %reshape.255), calls=%async_computation.5 | async-start | bytes 3538944 | tf_op jit(solution)/shard_map/all_to_all | solution.py:110
  488.4 6.7 %gather_fusion.1 = bf16[768]{0:T(1024)(128)(2,1)S(1)} fusion(bf16[16,256]{1,0:T(8,128)(2,1)S(1)} %fusion.22, s32[768]{0:T(1024)S(1)} %reshape.237), kind=kCustom, calls=%fused_computation.1 | custom fusion | bytes 9216 | tf_op jit(solution)/shard_map/jit(take_along_axis)/gather | solution.py:111
  495.2 35.0 %all-to-all-done.5 = bf16[16,2,27648]{2,1,0:T(2,128)(2,1)} async-done(((bf16[16,2,27648]{2,1,0:T(2,128)(2,1)}), bf16[16,2,27648]{2,1,0:T(2,128)(2,1)}, u32[]{:S(2)}, u32[]{:S(2)}) %all-to-all-start.5) | async-done | bytes 1769504 | tf_op jit(solution)/shard_map/all_to_all | solution.py:110
  530.2 10.0 %reshape.256 = bf16[768,1,1152]{2,1,0:T(2,128)(2,1)} reshape(bf16[16,2,27648]{2,1,0:T(2,128)(2,1)} %all-to-all-done.5) | data formatting | bytes 3538944
  (111 shorter events, 93.3 us)
Async XLA Ops:
  6.5 186.5 %copy-start = (bf16[1152,1152]{1,0:T(8,128)(2,1)S(1)}, bf16[1152,1152]{1,0:T(8,128)(2,1)}, u32[]{:S(2)}) copy-start(bf16[1152,1152]{1,0:T(8,128)(2,1)} %param.21) | copy-start | bytes 7962628
  8.8 18.6 %all-to-all-start = ((bf16[16,1,72,256]{3,2,1,0:T(8,128)(2,1)}), bf16[16,1,72,256]{3,2,1,0:T(8,128)(2,1)S(1)}, u32[]{:S(2)}, u32[]{:S(2)}) async-start(bf16[16,1,72,256]{3,2,1,0:T(8,128)(2,1)} %bitcast.139), calls=%async_computation | async-start | bytes 1179648 | tf_op jit(solution)/shard_map/all_to_all | solution.py:75
  27.4 18.5 %copy-start.5 = (s32[16,1,48]{2,1,0:T(1,128)S(1)}, s32[16,1,48]{2,1,0:T(1,128)}, u32[]{:S(2)}) copy-start(s32[16,1,48]{2,1,0:T(1,128)} %param.29) | copy-start | bytes 9220
  27.4 18.7 %copy-start.4 = (f32[1,4,1152]{2,1,0:T(4,128)S(1)}, f32[1,4,1152]{2,1,0:T(4,128)}, u32[]{:S(2)}) copy-start(f32[1,4,1152]{2,1,0:T(4,128)} %param.20) | copy-start | bytes 55300
  27.4 13.8 %all-to-all-start.1 = ((bf16[16,1,72,256]{3,2,1,0:T(8,128)(2,1)}), bf16[16,1,72,256]{3,2,1,0:T(8,128)(2,1)}, u32[]{:S(2)}, u32[]{:S(2)}) async-start(bf16[16,1,72,256]{3,2,1,0:T(8,128)(2,1)} %bitcast.138), calls=%async_computation.1 | async-start | bytes 1179648 | tf_op jit(solution)/shard_map/all_to_all | solution.py:76
  41.2 14.1 %all-to-all-start.2 = ((bf16[16,1,72,256]{3,2,1,0:T(8,128)(2,1)}), bf16[16,1,72,256]{3,2,1,0:T(8,128)(2,1)}, u32[]{:S(2)}, u32[]{:S(2)}) async-start(bf16[16,1,72,256]{3,2,1,0:T(8,128)(2,1)} %bitcast.137), calls=%async_computation.2 | async-start | bytes 1179648 | tf_op jit(solution)/shard_map/all_to_all | solution.py:77
  62.2 1.5 copy-start.2
  71.5 1.5 copy-start.2
  80.8 1.5 copy-start.2
  90.1 1.5 copy-start.2
  99.4 1.5 copy-start.2
  108.7 1.5 copy-start.2
  117.9 1.5 copy-start.2
  127.2 1.5 copy-start.2
  165.8 8.0 %copy-start.8 = (s32[16,1]{0,1:T(1,128)S(1)}, s32[16,1]{0,1:T(1,128)}, u32[]{:S(2)}) copy-start(s32[16,1]{0,1:T(1,128)} %param.28) | copy-start | bytes 196
  170.1 12.9 %all-to-all-start.3 = ((bf16[16,2,9216]{2,1,0:T(2,128)(2,1)}), bf16[16,2,9216]{2,1,0:T(2,128)(2,1)S(1)}, u32[]{:S(2)}, u32[]{:S(2)}) async-start(bf16[16,2,9216]{2,1,0:T(2,128)(2,1)} %reshape.253), calls=%async_computation.3 | async-start | bytes 1179648 | tf_op jit(solution)/shard_map/all_to_all | solution.py:80
  173.7 177.1 %all-reduce.3.cloned.1.call-start = ((), (), s32[]{:S(2)}) async-start(), calls=%async_computation.6 | async-start | bytes 3538944 | tf_op jit(solution)/shard_map/psum | solution.py:99
  192.7 1.1 copy-start.9
  192.7 1.1 copy-start.10
  194.9 1.0 copy-start.1
  259.6 195.4 %all-reduce.5.cloned.1.call-start = ((), (), s32[]{:S(2)}) async-start(), calls=%async_computation.7 | async-start | bytes 3538944 | tf_op jit(solution)/shard_map/psum | solution.py:108
  356.0 0.7 copy-start.6
  478.5 9.7 %copy-start.3 = (bf16[1152,16]{0,1:T(8,128)(2,1)S(1)}, bf16[1152,16]{0,1:T(8,128)(2,1)}, u32[]{:S(2)}) copy-start(bf16[1152,16]{0,1:T(8,128)(2,1)} %param.23) | copy-start | bytes 110596
  478.5 51.7 %all-to-all-start.5 = ((bf16[16,2,27648]{2,1,0:T(2,128)(2,1)}), bf16[16,2,27648]{2,1,0:T(2,128)(2,1)}, u32[]{:S(2)}, u32[]{:S(2)}) async-start(bf16[16,2,27648]{2,1,0:T(2,128)(2,1)} %reshape.255), calls=%async_computation.5 | async-start | bytes 3538944 | tf_op jit(solution)/shard_map/all_to_all | solution.py:110
  (1 other events, 0.7 us)
Sparse Core Ops, SparseCore 0:
  259.7 91.0 all-reduce.2
  356.2 98.7 all-reduce.4
where the time goes:
time: 553 us; the launch traced here: 551 us
  waiting for transfers between devices  256 us (46%)
  local copies, waits for them, and re-layouts  72.2 us (13%)
  blocking collectives  57.8 us (10%)
  other arithmetic  53.5 us (10%)
  matrix products  52.8 us (10%)
  starting transfers between devices  29.8 us (5%)
  loops' own time  15 us (3%)
  between operations  13.7 us (2%)
    psum x1, waiting for transfers between devices, per_device(): lax.psum(partial_out.astype(jnp.bfloat16), 'tok').astype(jnp.float32)  98.2 us
    psum x1, waiting for transfers between devices, per_device(): lax.psum(moved.astype(jnp.float32).astype(jnp.bfloat16), 'tok')  90.5 us
    all_to_all x1, blocking collectives, per_device(): lax.all_to_all(chosen, 'frame', split_axis=0, concat_axis=1, tiled=True)  57.8 us
    unnamed x32, local copies, waits for them, and re-layouts  37.8 us
    unnamed x4, other arithmetic  37 us
    all_to_all x1, waiting for transfers between devices, per_device(): lax.all_to_all(expert_out, 'frame', split_axis=1, concat_axis=0, tiled=True)  35 us
    dot_general x8, matrix products, one_block(): lax.dot_general(head_values, weights, (((1,), (1,)), ((), ())), preferred...  23.4 us
    dot_general x8, matrix products, one_block(): lax.dot_general(query_block, head_keys, (((0,), (0,)), ((), ())), preferr...  18.8 us
  transfers between devices with their start and end apart: 7, of which 7 were waited for; matrix products, arithmetic and copies ran while one was open for 3% of the time, Pallas kernels for 0%

commit v1 on v0

--- a/solution.py
+++ b/solution.py
@@ -105,7 +105,9 @@
     partial_out = jnp.einsum(
         "erf,efd->erd", hidden, reduce_weight, preferred_element_type=jnp.float32
     )
-    summed = lax.psum(partial_out.astype(jnp.bfloat16), "tok").astype(jnp.float32)
+    summed = jnp.sum(lax.all_gather(partial_out.astype(jnp.bfloat16), "tok"), axis=0).astype(
+        jnp.float32
+    )
     expert_out = (summed + reduce_bias[:, None, :]).astype(jnp.bfloat16)
     returned_rows = lax.all_to_all(expert_out, "frame", split_axis=1, concat_axis=0, tiled=True)
     mix_weight = jnp.take_along_axis(gate_values.T, safe_pos, axis=1)

time: 553 us -> 643 us (1.16)
  waiting for transfers between devices: 256 us -> 334 us
  other arithmetic: 53.5 us -> 70.9 us
    all_gather x0 -> x1, waiting for transfers between devices: none -> 176 us  [per_device(): lax.all_gather(partial_out.astype(jnp.bfloat16), 'tok')]
    psum x1 -> x0, waiting for transfers between devices: 98.2 us -> none  [per_device(): lax.psum(partial_out.astype(jnp.bfloat16), 'tok').astype(jnp.float32)]
    reduce_sum x0 -> x1, other arithmetic: none -> 11.6 us  [per_device(): jnp.sum(lax.all_gather(partial_out.astype(jnp.bfloat16), 'tok'), axis=0)]
    unnamed x4 -> x5, other arithmetic: 37 us -> 42.9 us
  transfers between devices with their start and end apart: 7 -> 7, of which waited for: 7 -> 7; matrix products, arithmetic and copies ran while one was open for 3% -> 2% of each run, Pallas kernels for 0% -> 0%
where the time goes in v1:
time: 643 us; the launch traced here: 641 us
  waiting for transfers between devices  334 us (52%)
  other arithmetic  70.9 us (11%)
  local copies, waits for them, and re-layouts  69 us (11%)
  blocking collectives  57.8 us (9%)
  matrix products  52.9 us (8%)
  starting transfers between devices  28.2 us (4%)
  loops' own time  15 us (2%)
  between operations  13.7 us (2%)
    all_gather x1, waiting for transfers between devices, per_device(): lax.all_gather(partial_out.astype(jnp.bfloat16), 'tok')  176 us
    psum x1, waiting for transfers between devices, per_device(): lax.psum(moved.astype(jnp.float32).astype(jnp.bfloat16), 'tok')  90.5 us
    all_to_all x1, blocking collectives, per_device(): lax.all_to_all(chosen, 'frame', split_axis=0, concat_axis=1, tiled=True)  57.8 us
    unnamed x5, other arithmetic  42.9 us
    unnamed x32, local copies, waits for them, and re-layouts  38.4 us
    all_to_all x1, waiting for transfers between devices, per_device(): lax.all_to_all(expert_out, 'frame', split_axis=1, concat_axis=0, tiled=True)  35 us
    dot_general x8, matrix products, one_block(): lax.dot_general(head_values, weights, (((1,), (1,)), ((), ())), preferred...  23.4 us
    dot_general x8, matrix products, one_block(): lax.dot_general(query_block, head_keys, (((0,), (0,)), ((), ())), preferr...  18.8 us
  transfers between devices with their start and end apart: 7, of which 7 were waited for; matrix products, arithmetic and copies ran while one was open for 2% of the time, Pallas kernels for 0%

profile of v1, /device:TPU:1, one launch (start us, length us, event | category | flops | bytes accessed | tf_op | source)
XLA Modules:
  0.0 640.9 jit_solution(18432811998688639279)
XLA Ops:
  8.8 7.6 %all-to-all-start = ((bf16[16,1,72,256]{3,2,1,0:T(8,128)(2,1)}), bf16[16,1,72,256]{3,2,1,0:T(8,128)(2,1)S(1)}, u32[]{:S(2)}, u32[]{:S(2)}) async-start(bf16[16,1,72,256]{3,2,1,0:T(8,128)(2,1)} %bitcast.136), calls=%async_computation | async-start | bytes 1179648 | tf_op jit(solution)/shard_map/all_to_all | solution.py:75
  18.5 8.9 %all-to-all-done = bf16[16,1,72,256]{3,2,1,0:T(8,128)(2,1)S(1)} async-done(((bf16[16,1,72,256]{3,2,1,0:T(8,128)(2,1)}), bf16[16,1,72,256]{3,2,1,0:T(8,128)(2,1)S(1)}, u32[]{:S(2)}, u32[]{:S(2)}) %all-to-all-start) | async-done | bytes 589856 | tf_op jit(solution)/shard_map/all_to_all | solution.py:75
  27.4 4.4 all-to-all-start.1
  33.9 7.3 %all-to-all-done.1 = bf16[16,1,72,256]{3,2,1,0:T(8,128)(2,1)} async-done(((bf16[16,1,72,256]{3,2,1,0:T(8,128)(2,1)}), bf16[16,1,72,256]{3,2,1,0:T(8,128)(2,1)}, u32[]{:S(2)}, u32[]{:S(2)}) %all-to-all-start.1) | async-done | bytes 589856 | tf_op jit(solution)/shard_map/all_to_all | solution.py:76
  41.2 4.7 all-to-all-start.2
  48.1 7.2 %all-to-all-done.2 = bf16[16,1,72,256]{3,2,1,0:T(8,128)(2,1)} async-done(((bf16[16,1,72,256]{3,2,1,0:T(8,128)(2,1)}), bf16[16,1,72,256]{3,2,1,0:T(8,128)(2,1)}, u32[]{:S(2)}, u32[]{:S(2)}) %all-to-all-start.2) | async-done | bytes 589856 | tf_op jit(solution)/shard_map/all_to_all | solution.py:77
  57.3 74.4 %while.17 = (s32[]{:T(128)}, bf16[8,72,512]{2,1,0:T(8,128)(2,1)}, s32[8]{0:T(128)S(1)}, bf16[72,4096]{1,0:T(8,128)(2,1)}, bf16[72,4096]{1,0:T(8,128)(2,1)S(1)}, ...) while((s32[]{:T(128)}, bf16[8,72,512]{2,1,0:T(8,128)(2,1)}, s32[8]{0:T(128)S(1)}, ...), condition=%wide.region_3.0_spmd, body=%wide.region_0.3_spmd.sunk | while | flops 622889984 | bytes 28863148 | solution.py:40
  133.9 6.9 %reshape.292 = bf16[1,1,72,4096]{2,1,0,3:T(2,128)(2,1)} reshape(bf16[72,8,512]{0,2,1:T(8,128)(2,1)} %copy.76) | data formatting | bytes 1179648 | tf_op jit(solution)/shard_map/broadcast_in_dim | solution.py:46
  141.3 24.5 %reduce.15 = bf16[4096,72]{1,0:T(8,128)(2,1)} reduce(bf16[4096,1,1,72]{3,2,1,0:T(2,128)(2,1)} %bitcast.128, bf16[]{:T(256)} %broadcast.295), dimensions={1,2}, to_apply=%bitcast.106.reduce_sub_computation | reduce | bytes 1179650
  173.9 9.1 %all-to-all-done.3 = bf16[16,2,9216]{2,1,0:T(2,128)(2,1)S(1)} async-done(((bf16[16,2,9216]{2,1,0:T(2,128)(2,1)}), bf16[16,2,9216]{2,1,0:T(2,128)(2,1)S(1)}, u32[]{:S(2)}, u32[]{:S(2)}) %all-to-all-start.3) | async-done | bytes 589856 | tf_op jit(solution)/shard_map/all_to_all | solution.py:80
  183.0 5.1 reshape.304
  188.1 5.2 copy.72
  202.9 57.8 %all_to_all.84 = bf16[16,48,1152]{2,1,0:T(8,128)(2,1)} all-to-all(bf16[16,48,1152]{2,1,0:T(8,128)(2,1)S(1)} %select_select_fusion), channel_id=1, replica_groups=mesh['frame'=16,'tok'=16] {'frame'}, dimensions={0} | all-to-all | bytes 3538944 | tf_op jit(solution)/shard_map/all_to_all | solution.py:98
  261.3 90.5 %all-reduce.2.cloned.1.call-done = bf16[768,1152]{1,0:T(8,128)(2,1)} async-done(((bf16[768,1152]{1,0:T(8,128)(2,1)}), bf16[768,1152]{1,0:T(8,128)(2,1)}) %all-reduce.2.cloned.1.call-update) | async-done | bytes 1769488 | tf_op jit(solution)/shard_map/psum | solution.py:99
  351.9 5.4 convolution_convert_fusion
  357.9 175.5 %all-gather.3.cloned.1.call-done = bf16[12288,1152]{1,0:T(8,128)(2,1)} async-done(((bf16[768,1152]{1,0:T(8,128)(2,1)}), bf16[12288,1152]{1,0:T(8,128)(2,1)}) %all-gather.3.cloned.1.call-update) | async-done | bytes 28311568 | tf_op jit(solution)/shard_map/all_gather | solution.py:108
  533.5 11.6 %reduce.2 = bf16[768,1152]{1,0:T(8,128)(2,1)} reduce(bf16[16,768,1152]{2,1,0:T(8,128)(2,1)} %bitcast.126, bf16[]{:T(256)} %constant.42.clone.1), dimensions={0}, to_apply=%region_7.8 | reduce | flops 13271040 | bytes 30081026 | tf_op jit(solution)/shard_map/reduce_sum | solution.py:108
  546.8 5.8 fusion.53
  552.6 12.6 %reduce.16 = bf16[768,1152]{1,0:T(8,128)(2,1)} reduce(bf16[768,1,1152]{2,1,0:T(2,128)(2,1)} %fusion.53, bf16[]{:T(256)} %broadcast.295), dimensions={1}, to_apply=%fusion.53.reduce_sub_computation | reduce | bytes 3538946
  565.2 4.7 reshape.305
  569.8 7.8 %all-to-all-start.5 = ((bf16[16,2,27648]{2,1,0:T(2,128)(2,1)}), bf16[16,2,27648]{2,1,0:T(2,128)(2,1)}, u32[]{:S(2)}, u32[]{:S(2)}) async-start(bf16[16,2,27648]{2,1,0:T(2,128)(2,1)} %reshape.305), calls=%async_computation.5 | async-start | bytes 3538944 | tf_op jit(solution)/shard_map/all_to_all | solution.py:112
  578.4 6.7 %gather_fusion.1 = bf16[768]{0:T(1024)(128)(2,1)S(1)} fusion(bf16[16,256]{1,0:T(8,128)(2,1)S(1)} %fusion.22, s32[768]{0:T(1024)S(1)} %reshape.282), kind=kCustom, calls=%fused_computation.1 | custom fusion | bytes 9216 | tf_op jit(solution)/shard_map/jit(take_along_axis)/gather | solution.py:113
  585.2 35.0 %all-to-all-done.5 = bf16[16,2,27648]{2,1,0:T(2,128)(2,1)} async-done(((bf16[16,2,27648]{2,1,0:T(2,128)(2,1)}), bf16[16,2,27648]{2,1,0:T(2,128)(2,1)}, u32[]{:S(2)}, u32[]{:S(2)}) %all-to-all-start.5) | async-done | bytes 1769504 | tf_op jit(solution)/shard_map/all_to_all | solution.py:112
  620.2 10.0 %reshape.306 = bf16[768,1,1152]{2,1,0:T(2,128)(2,1)} reshape(bf16[16,2,27648]{2,1,0:T(2,128)(2,1)} %all-to-all-done.5) | data formatting | bytes 3538944
  (112 shorter events, 97.9 us)
Async XLA Ops:
  6.5 188.3 %copy-start = (bf16[1152,1152]{1,0:T(8,128)(2,1)S(1)}, bf16[1152,1152]{1,0:T(8,128)(2,1)}, u32[]{:S(2)}) copy-start(bf16[1152,1152]{1,0:T(8,128)(2,1)} %param.21) | copy-start | bytes 7962628
  8.8 18.6 %all-to-all-start = ((bf16[16,1,72,256]{3,2,1,0:T(8,128)(2,1)}), bf16[16,1,72,256]{3,2,1,0:T(8,128)(2,1)S(1)}, u32[]{:S(2)}, u32[]{:S(2)}) async-start(bf16[16,1,72,256]{3,2,1,0:T(8,128)(2,1)} %bitcast.136), calls=%async_computation | async-start | bytes 1179648 | tf_op jit(solution)/shard_map/all_to_all | solution.py:75
  27.4 18.5 %copy-start.5 = (s32[16,1,48]{2,1,0:T(1,128)S(1)}, s32[16,1,48]{2,1,0:T(1,128)}, u32[]{:S(2)}) copy-start(s32[16,1,48]{2,1,0:T(1,128)} %param.29) | copy-start | bytes 9220
  27.4 18.7 %copy-start.4 = (f32[1,4,1152]{2,1,0:T(4,128)S(1)}, f32[1,4,1152]{2,1,0:T(4,128)}, u32[]{:S(2)}) copy-start(f32[1,4,1152]{2,1,0:T(4,128)} %param.20) | copy-start | bytes 55300
  27.4 13.8 %all-to-all-start.1 = ((bf16[16,1,72,256]{3,2,1,0:T(8,128)(2,1)}), bf16[16,1,72,256]{3,2,1,0:T(8,128)(2,1)}, u32[]{:S(2)}, u32[]{:S(2)}) async-start(bf16[16,1,72,256]{3,2,1,0:T(8,128)(2,1)} %bitcast.135), calls=%async_computation.1 | async-start | bytes 1179648 | tf_op jit(solution)/shard_map/all_to_all | solution.py:76
  41.2 14.1 %all-to-all-start.2 = ((bf16[16,1,72,256]{3,2,1,0:T(8,128)(2,1)}), bf16[16,1,72,256]{3,2,1,0:T(8,128)(2,1)}, u32[]{:S(2)}, u32[]{:S(2)}) async-start(bf16[16,1,72,256]{3,2,1,0:T(8,128)(2,1)} %bitcast.134), calls=%async_computation.2 | async-start | bytes 1179648 | tf_op jit(solution)/shard_map/all_to_all | solution.py:77
  62.2 1.5 copy-start.2
  71.5 1.5 copy-start.2
  80.8 1.5 copy-start.2
  90.1 1.5 copy-start.2
  99.4 1.5 copy-start.2
  108.7 1.5 copy-start.2
  117.9 1.5 copy-start.2
  127.2 1.5 copy-start.2
  165.8 8.0 %copy-start.8 = (s32[16,1]{0,1:T(1,128)S(1)}, s32[16,1]{0,1:T(1,128)}, u32[]{:S(2)}) copy-start(s32[16,1]{0,1:T(1,128)} %param.28) | copy-start | bytes 196
  170.2 12.9 %all-to-all-start.3 = ((bf16[16,2,9216]{2,1,0:T(2,128)(2,1)}), bf16[16,2,9216]{2,1,0:T(2,128)(2,1)S(1)}, u32[]{:S(2)}, u32[]{:S(2)}) async-start(bf16[16,2,9216]{2,1,0:T(2,128)(2,1)} %reshape.303), calls=%async_computation.3 | async-start | bytes 1179648 | tf_op jit(solution)/shard_map/all_to_all | solution.py:80
  173.7 178.1 %all-reduce.2.cloned.1.call-start = ((), (), s32[]{:S(2)}) async-start(), calls=%async_computation.6 | async-start | bytes 3538944 | tf_op jit(solution)/shard_map/psum | solution.py:99
  193.4 1.5 copy-start.9
  193.4 1.5 copy-start.10
  196.0 1.0 copy-start.1
  260.7 272.8 %all-gather.3.cloned.1.call-start = ((), (), s32[]{:S(2)}) async-start(), calls=%async_computation.7 | async-start | bytes 30081024 | tf_op jit(solution)/shard_map/all_gather | solution.py:108
  357.2 0.7 copy-start.6
  569.8 8.3 %copy-start.3 = (bf16[1152,16]{0,1:T(8,128)(2,1)S(1)}, bf16[1152,16]{0,1:T(8,128)(2,1)}, u32[]{:S(2)}) copy-start(bf16[1152,16]{0,1:T(8,128)(2,1)} %param.23) | copy-start | bytes 110596
  569.8 50.3 %all-to-all-start.5 = ((bf16[16,2,27648]{2,1,0:T(2,128)(2,1)}), bf16[16,2,27648]{2,1,0:T(2,128)(2,1)}, u32[]{:S(2)}, u32[]{:S(2)}) async-start(bf16[16,2,27648]{2,1,0:T(2,128)(2,1)} %reshape.305), calls=%async_computation.5 | async-start | bytes 3538944 | tf_op jit(solution)/shard_map/all_to_all | solution.py:112
  (1 other events, 0.7 us)
Sparse Core Ops, SparseCore 0:
  260.8 91.0 all-reduce.1
  357.4 176.0 all-gather.2
